TPU v7x, 512 devices: a whole 4x4x16 slice. The times are simulated.
512 devices in a mesh: dp: 64 (over y_hi, z, core), tensor: 8 (over x, y_lo).
Axes of the slice: x: 4, y: 4 (y_hi: 2, y_lo: 2; y = y_hi * 2 + y_lo), z: 16, core: 2. Of those that a mesh axis runs over, the one named last changes fastest.
Arguments:
- queries: bfloat16 [2048, 5120], P('dp', 'tensor'), may hold values from -8 to 8
- new_keys: bfloat16 [2048, 5120], P('dp', 'tensor'), may hold values from -8 to 8
- new_values: bfloat16 [2048, 5120], P('dp', 'tensor'), may hold values from -6 to 6
- key_pool: bfloat16 [1024, 16, 5120], P('dp', None, 'tensor'), may hold values from -6 to 6
- value_pool: bfloat16 [1024, 16, 5120], P('dp', None, 'tensor'), may hold values from -6 to 6
- page_table: int32 [128, 16], P('dp'), may hold values from 0 to 15, as said below
- lengths: int32 [128], P('dp'), may hold values from 1 to 240, as said below
- timesteps: int32 [128], replicated, may hold values from 0 to 49
- gate_table: float32 [50, 5120], P(None, 'dp'), may hold values from -4 to 4
- out_weight: bfloat16 [5120, 5120], P('tensor', 'dp'), may hold values from -0.078125 to 0.078125
- residual: bfloat16 [32, 64, 5120], P('tensor', None, 'dp'), may hold values from -1.5 to 1.5
Outputs:
- mixed: bfloat16 [32, 64, 5120], P('tensor', None, 'dp')
Inputs may be any that keep to these rules, and one draw needn't show every extreme that they name: `page_table`: ids of pages within the 16-page pool of the request's own group; the first ceil(lengths[r] / 16) entries of the requests of one group are distinct pages, and together they take at most 16 pages; in every draw some group takes all 16. `lengths`: some request has exactly 240 cached positions in every draw.
All inputs are finite; a program needn't handle non-finite values.
Results may differ from a plain program's by a relative error of at most 0.0054.
Values may be sent and summed in bfloat16 or wider, within the bound.
No kernel may reach another device: no remote copies, remote signals or barrier semaphores. Data moves between devices by JAX's collectives and lax.ppermute only.
A program may use at most 64 MiB of HBM per device.

v0:
```python
import math

import jax
import jax.numpy as jnp
from jax import lax
from jax.sharding import PartitionSpec as P

HEAD = 128


def attend(queries, new_keys, new_values, key_pool, value_pool, page_table, lengths):
    req_dev = page_table.shape[0]
    pages, page_len, width = key_pool.shape
    tok_count = queries.shape[0]
    new_count = tok_count // req_dev
    heads_dev = width // HEAD
    cached = pages * page_len
    keys_all = jnp.concatenate(
        [
            key_pool[page_table].reshape(req_dev, cached, width),
            new_keys.reshape(req_dev, new_count, width),
        ],
        axis=1,
    )
    vals_all = jnp.concatenate(
        [
            value_pool[page_table].reshape(req_dev, cached, width),
            new_values.reshape(req_dev, new_count, width),
        ],
        axis=1,
    )
    keys_all = keys_all.reshape(req_dev, cached + new_count, heads_dev, HEAD)
    vals_all = vals_all.reshape(req_dev, cached + new_count, heads_dev, HEAD)
    query_four = queries.reshape(req_dev, new_count, heads_dev, HEAD)
    scores = jnp.einsum(
        "rqhd,rkhd->rhqk", query_four, keys_all, preferred_element_type=jnp.float32
    ) * (1.0 / math.sqrt(HEAD))
    position = jnp.arange(cached + new_count)
    visible = (position[None, :] < lengths[:, None]) | (position[None, :] >= cached)
    scores = jnp.where(visible[:, None, None, :], scores, jnp.float32(-1e30))
    top = jnp.max(scores, axis=-1, keepdims=True)
    expd = jnp.exp(scores - top)
    probs = (expd / jnp.sum(expd, axis=-1, keepdims=True)).astype(jnp.bfloat16)
    mixed_heads = jnp.einsum("rhqk,rkhd->rqhd", probs, vals_all, preferred_element_type=jnp.float32)
    return mixed_heads.astype(jnp.bfloat16).reshape(tok_count, width)


def per_device(
    queries,
    new_keys,
    new_values,
    key_pool,
    value_pool,
    page_table,
    lengths,
    timesteps,
    gate_table,
    out_weight,
    residual,
):
    attn = attend(queries, new_keys, new_values, key_pool, value_pool, page_table, lengths)
    group_tok = attn.shape[0]
    req_dev = page_table.shape[0]
    new_count = group_tok // req_dev
    share = residual.shape[0]
    groups = residual.shape[1]
    col_count = out_weight.shape[1]
    partial_all = jnp.dot(
        attn,
        lax.all_gather(out_weight, "dp", axis=1, tiled=True),
        preferred_element_type=jnp.float32,
    )
    blocks = partial_all.reshape(group_tok, groups, col_count)
    regrouped = lax.all_to_all(blocks, "dp", split_axis=1, concat_axis=1, tiled=True)
    branch = lax.psum_scatter(regrouped, "tensor", scatter_dimension=0, tiled=True)
    tensor_at = lax.axis_index("tensor")
    local_rows = tensor_at * share + jnp.arange(share, dtype=jnp.int32)
    request_at = (
        jnp.arange(groups, dtype=jnp.int32)[None, :] * req_dev + (local_rows // new_count)[:, None]
    )
    step_at = timesteps[request_at]
    onehot = (
        step_at[:, :, None] == jnp.arange(gate_table.shape[0], dtype=jnp.int32)[None, None, :]
    ).astype(jnp.float32)
    gate = jnp.einsum("tgs,sc->tgc", onehot, gate_table, precision=lax.Precision.HIGHEST)
    return (residual.astype(jnp.float32) + gate * branch).astype(jnp.bfloat16)


def solution(mesh):
    placed = (
        P("dp", "tensor"),
        P("dp", "tensor"),
        P("dp", "tensor"),
        P("dp", None, "tensor"),
        P("dp", None, "tensor"),
        P("dp", None),
        P("dp"),
        P(),
        P(None, "dp"),
        P("tensor", "dp"),
        P("tensor", None, "dp"),
    )
    return jax.shard_map(
        per_device, mesh=mesh, in_specs=placed, out_specs=P("tensor", None, "dp"), check_vma=False
    )
```

profile of v0, /device:TPU:1, one launch (start us, length us, event | category | flops | bytes accessed | tf_op | source)
XLA Modules:
  0.0 289.5 jit_solution(7618827697178284164)
XLA Ops:
  6.5 0.0 copy-start
  6.5 0.0 all-gather.2.cloned.1.call-start
  6.5 0.7 all-gather.2.cloned.1.call-update
  7.3 0.0 reduce-scatter.2.cloned.1.call-start
  7.3 0.7 compare_select_fusion.1
  8.0 0.1 reshape.147
  8.1 0.0 copy-done
  8.1 0.7 gather_fusion.2
  8.8 0.0 copy-start.4
  8.8 0.0 copy-start.5
  8.8 0.7 concatenate.19
  9.5 0.0 copy-start.2
  9.5 0.1 copy.23
  9.6 0.0 copy-done.4
  9.6 0.1 concatenate.20
  9.7 0.0 copy-done.5
  9.7 0.1 reshape.135
  9.8 0.7 copy-done.2
  10.5 0.7 gather_fusion.1
  11.2 0.0 copy-start.6
  11.2 0.0 copy-start.8
  11.2 0.7 concatenate.16
  11.9 0.1 copy.21
  12.0 0.0 copy-done.6
  12.1 0.1 concatenate.17
  12.2 0.0 copy-done.8
  12.2 0.1 compare_or_fusion
  12.2 0.5 fusion.48
  12.7 0.5 fusion.7
  13.3 0.1 reshape.169
  13.4 161.4 %all-gather.2.cloned.1.call-done = bf16[640,5120]{0,1:T(8,128)(2,1)} async-done(((bf16[640,80]{0,1:T(8,128)(2,1)}), bf16[640,5120]{0,1:T(8,128)(2,1)}) %all-gather.2.cloned.1.call-update) | async-done | bytes 6553616 | tf_op jit(solution)/shard_map/all_gather | solution.py:70
  174.9 5.9 %fusion.53 = f32[32,64,80]{2,0,1:T(8,128)S(1)} fusion(bf16[32,640,1]{1,0,2:T(8,128)(2,1)S(1)} %reshape.169, bf16[64,80,640]{2,1,0:T(8,128)(2,1)} %bitcast.24), kind=kOutput, calls=%fused_computation.47 | convolution fusion | flops 209715200 | bytes 7249920 | tf_op jit(solution)/shard_map/dot_general | solution.py:68
  180.8 59.3 %all_to_all.5 = f32[32,64,80]{2,0,1:T(8,128)S(1)} all-to-all(f32[32,64,80]{2,0,1:T(8,128)S(1)} %fusion.53), channel_id=1, replica_groups=mesh['dp'=64,'tensor'=8] {'dp'}, dimensions={1} | all-to-all | bytes 1310720 | tf_op jit(solution)/shard_map/all_to_all | solution.py:74
  240.1 0.0 copy-start.1
  240.1 1.6 copy.27
  241.7 0.0 copy-start.3
  241.7 0.0 copy-start.7
  241.7 0.0 reduce-scatter.2.cloned.1.call-update
  241.7 0.1 compare_select_fusion
  241.8 0.1 reshape.139
  241.9 0.0 copy-done.1
  241.9 1.9 gather_fusion
  243.8 0.1 reshape.138
  243.9 37.0 %reduce-scatter.2.cloned.1.call-done = f32[4,64,80]{2,1,0:T(8,128)} async-done(((f32[32,64,80]{2,1,0:T(8,128)}), f32[4,64,80]{2,1,0:T(8,128)}) %reduce-scatter.2.cloned.1.call-update) | async-done | bytes 81936 | tf_op jit(solution)/shard_map/reduce_scatter | solution.py:75
  280.8 0.0 copy-done.3
  280.8 0.0 copy-done.7
  280.8 1.8 fusion.6
  (8 shorter events, 0.1 us)
Async XLA Ops:
  6.5 1.5 copy-start
  6.5 168.3 %all-gather.2.cloned.1.call-start = ((), (), s32[]{:S(2)}) async-start(), calls=%async_computation.2 | async-start | bytes 6656000 | tf_op jit(solution)/shard_map/all_gather | solution.py:70
  7.3 273.6 %reduce-scatter.2.cloned.1.call-start = ((), (), s32[]{:S(2)}) async-start(), calls=%async_computation.3 | async-start | bytes 1179648 | tf_op jit(solution)/shard_map/reduce_scatter | solution.py:75
  8.8 0.9 copy-start.4
  8.8 1.0 copy-start.5
  9.5 1.0 copy-start.2
  11.2 0.9 copy-start.6
  11.2 1.0 copy-start.8
  240.1 1.8 copy-start.1
  241.7 39.2 %copy-start.3 = (bf16[4,64,80]{2,1,0:T(8,128)(2,1)S(1)}, bf16[4,64,80]{2,1,0:T(8,128)(2,1)}, u32[]{:S(2)}) copy-start(bf16[4,64,80]{2,1,0:T(8,128)(2,1)} %param.21) | copy-start | bytes 122884
  241.7 39.2 %copy-start.7 = (f32[50,80]{1,0:T(8,128)S(1)}, f32[50,80]{1,0:T(8,128)}, u32[]{:S(2)}) copy-start(f32[50,80]{1,0:T(8,128)} %param.19) | copy-start | bytes 48004
Sparse Core Ops, SparseCore 0:
  10.4 164.4 all-gather.1
  241.8 38.9 reduce-scatter.1
where the time goes:
time: 293 us; the launch traced here: 290 us
  waiting for transfers between devices  199 us (68%)
  blocking collectives  59.3 us (20%)
  between operations  13.6 us (5%)
  matrix products  8.78 us (3%)
  local copies, waits for them, and re-layouts  7.73 us (3%)
    all_gather x1, waiting for transfers between devices, per_device(): lax.all_gather(out_weight, 'dp', axis=1, tiled=True)  161 us
    all_to_all x1, blocking collectives, per_device(): lax.all_to_all(blocks, 'dp', split_axis=1, concat_axis=1, tiled=True)  59.3 us
    reduce_scatter x1, waiting for transfers between devices, per_device(): lax.psum_scatter(regrouped, 'tensor', scatter_dimension=0, tiled=True)  37 us
    dot_general x1, matrix products, per_device(): jnp.dot(attn, lax.all_gather(out_weight, 'dp', axis=1, tiled=True), prefe...  5.9 us
  transfers between devices with their start and end apart: 2, of which 2 were waited for; matrix products, arithmetic and copies ran while one was open for 3% of the time, Pallas kernels for 0%

commit v1 on v0

--- a/solution.py
+++ b/solution.py
@@ -3,6 +3,7 @@
 import jax
 import jax.numpy as jnp
 from jax import lax
+from jax.sharding import Mesh
 from jax.sharding import PartitionSpec as P
 
 HEAD = 128
@@ -58,22 +59,25 @@
     out_weight,
     residual,
 ):
-    attn = attend(queries, new_keys, new_values, key_pool, value_pool, page_table, lengths)
-    group_tok = attn.shape[0]
     req_dev = page_table.shape[0]
+    group_tok = queries.shape[0]
     new_count = group_tok // req_dev
     share = residual.shape[0]
     groups = residual.shape[1]
     col_count = out_weight.shape[1]
-    partial_all = jnp.dot(
-        attn,
-        lax.all_gather(out_weight, "dp", axis=1, tiled=True),
-        preferred_element_type=jnp.float32,
-    )
-    blocks = partial_all.reshape(group_tok, groups, col_count)
-    regrouped = lax.all_to_all(blocks, "dp", split_axis=1, concat_axis=1, tiled=True)
-    branch = lax.psum_scatter(regrouped, "tensor", scatter_dimension=0, tiled=True)
-    tensor_at = lax.axis_index("tensor")
+    y_hi, z_len, cores = (lax.axis_size(name) for name in ("y_hi", "z", "core"))
+    tensor_len = lax.axis_size("x") * lax.axis_size("y_lo")
+    weight = lax.all_gather(out_weight, ("y_hi", "core"), axis=1, tiled=True)
+    attn = attend(queries, new_keys, new_values, key_pool, value_pool, page_table, lengths)
+    attn_all = lax.all_gather(attn, "z", axis=0, tiled=True)
+    partial = jnp.dot(attn_all, weight, preferred_element_type=jnp.float32).astype(jnp.bfloat16)
+    blocks = partial.reshape(z_len, tensor_len, share, y_hi * cores, col_count)
+    blocks = blocks.transpose(3, 1, 0, 2, 4).reshape(-1, z_len, share, col_count)
+    arrived = lax.all_to_all(blocks, ("y_hi", "core", "x", "y_lo"), 0, 0, tiled=True)
+    arrived = arrived.reshape(y_hi, cores, tensor_len, z_len, share, col_count)
+    branch = jnp.sum(arrived.astype(jnp.float32), axis=2)
+    branch = branch.transpose(3, 0, 2, 1, 4).reshape(share, groups, col_count)
+    tensor_at = lax.axis_index(("x", "y_lo"))
     local_rows = tensor_at * share + jnp.arange(share, dtype=jnp.int32)
     request_at = (
         jnp.arange(groups, dtype=jnp.int32)[None, :] * req_dev + (local_rows // new_count)[:, None]
@@ -87,19 +91,22 @@
 
 
 def solution(mesh):
+    dp = ("y_hi", "z", "core")
+    tensor = ("x", "y_lo")
+    split = Mesh(mesh.devices.reshape(2, -1, 2, 4, 2), dp + tensor)
     placed = (
-        P("dp", "tensor"),
-        P("dp", "tensor"),
-        P("dp", "tensor"),
-        P("dp", None, "tensor"),
-        P("dp", None, "tensor"),
-        P("dp", None),
-        P("dp"),
+        P(dp, tensor),
+        P(dp, tensor),
+        P(dp, tensor),
+        P(dp, None, tensor),
+        P(dp, None, tensor),
+        P(dp, None),
+        P(dp),
         P(),
-        P(None, "dp"),
-        P("tensor", "dp"),
-        P("tensor", None, "dp"),
+        P(None, dp),
+        P(tensor, dp),
+        P(tensor, None, dp),
     )
     return jax.shard_map(
-        per_device, mesh=mesh, in_specs=placed, out_specs=P("tensor", None, "dp"), check_vma=False
+        per_device, mesh=split, in_specs=placed, out_specs=P(tensor, None, dp), check_vma=False
     )

time: 293 us -> 78.3 us (0.27); the launches traced: 290 us -> 78 us
  waiting for transfers between devices: 199 us -> 9 us
  between operations: 13.6 us -> 0.25 us
  blocking collectives: 59.3 us -> 49.2 us
  starting transfers between devices: 0.04 us -> 6.7 us
  matrix products: 8.78 us -> 2.43 us
    all_gather x1 -> x0, waiting for transfers between devices: 161 us -> none  [per_device(): lax.all_gather(out_weight, 'dp', axis=1, tiled=True)]
    all_to_all x1 -> x0, blocking collectives: 59.3 us -> none  [per_device(): lax.all_to_all(blocks, 'dp', split_axis=1, concat_axis=1, tiled=True)]
    all_gather x0 -> x2, blocking collectives: none -> 49.2 us  [the longest x1 33.5 us: per_device(): attn_all = lax.all_gather(attn, 'z', axis=0, tiled=True)]
    reduce_scatter x1 -> x0, waiting for transfers between devices: 37 us -> none  [per_device(): lax.psum_scatter(regrouped, 'tensor', scatter_dimension=0, tiled=True)]
    all_to_all x0 -> x1, waiting for transfers between devices: none -> 9 us  [per_device(): lax.all_to_all(blocks, ('y_hi', 'core', 'x', 'y_lo'), 0, 0, tiled=True)]
    all_to_all x0 -> x1, starting transfers between devices: none -> 6.7 us  [per_device(): lax.all_to_all(blocks, ('y_hi', 'core', 'x', 'y_lo'), 0, 0, tiled=True)]
    dot_general x1, matrix products: 5.9 us -> 0.45 us  [per_device(): jnp.dot(attn_all, weight, preferred_element_type=jnp.float32)]
  transfers between devices with their start and end apart: 2 -> 1, of which waited for: 2 -> 1; matrix products, arithmetic and copies ran while one was open for 3% -> 3% of each run, Pallas kernels for 0% -> 0%
where the time goes in v1:
time: 78.3 us; the launch traced here: 78 us
  blocking collectives  49.2 us (63%)
  local copies, waits for them, and re-layouts  9.43 us (12%)
  waiting for transfers between devices  9 us (11%)
  starting transfers between devices  6.7 us (9%)
  matrix products  2.43 us (3%)
  other arithmetic  0.98 us (1%)
    all_gather x1, blocking collectives, per_device(): attn_all = lax.all_gather(attn, 'z', axis=0, tiled=True)  33.5 us
    all_gather x1, blocking collectives, per_device(): weight = lax.all_gather(out_weight, ('y_hi', 'core'), axis=1, tiled=True)  15.7 us
    all_to_all x1, waiting for transfers between devices, per_device(): lax.all_to_all(blocks, ('y_hi', 'core', 'x', 'y_lo'), 0, 0, tiled=True)  9 us
    all_to_all x1, starting transfers between devices, per_device(): lax.all_to_all(blocks, ('y_hi', 'core', 'x', 'y_lo'), 0, 0, tiled=True)  6.7 us
    gather x2, local copies, waits for them, and re-layouts, per_device(): step_at = timesteps[request_at]  1.95 us
    concatenate x4, local copies, waits for them, and re-layouts, attend(): jnp.concatenate([value_pool[page_table].reshape(req_dev, cached, width),...  1.73 us
  transfers between devices with their start and end apart: 1, of which 1 were waited for; matrix products, arithmetic and copies ran while one was open for 3% of the time, Pallas kernels for 0%

profile of v1, /device:TPU:1, one launch (start us, length us, event | category | flops | bytes accessed | tf_op | source)
XLA Modules:
  0.0 78.0 jit_solution(498488600279138065)
XLA Ops:
  0.0 0.0 copy-start
  0.0 0.9 %concatenate.17 = bf16[2,16,5,128]{3,2,1,0:T(8,128)(2,1)S(1)} reshape(bf16[32,640]{1,0:T(8,128)(2,1)} %param.13) | data formatting | bytes 81920 | tf_op jit(solution)/shard_map/concatenate | solution.py:26
  0.9 0.7 compare_select_fusion.1
  1.6 0.1 reshape.161
  1.7 0.0 copy-done
  1.7 0.7 gather_fusion.1
  2.4 0.7 concatenate.16
  3.1 0.0 copy-start.5
  3.1 0.0 copy-start.2
  3.1 0.1 copy.21
  3.2 0.6 copy-done.5
  3.9 0.1 concatenate.20
  4.0 0.1 copy-done.2
  4.1 0.7 gather_fusion.2
  4.8 0.7 concatenate.19
  5.5 0.0 copy-start.6
  5.5 0.0 copy-start.8
  5.5 0.1 copy.23
  5.6 0.6 copy-done.6
  6.3 0.1 reshape.145
  6.4 0.0 copy-done.8
  6.4 0.1 compare_or_fusion
  6.4 0.5 fusion.48
  6.9 0.0 copy-start.3
  6.9 0.6 fusion.7
  7.6 33.5 %all_gather.6 = bf16[512,640]{1,0:T(8,128)(2,1)S(1)} all-gather(bf16[32,640]{1,0:T(8,128)(2,1)S(1)} %bitcast.37), channel_id=1, replica_groups=mesh['y_hi'=2,'z'=16,'core'=2,'x'=4,'y_lo'=2] {'z'}, dimensions={0}, use_global_device_ids=true | all-gather | bytes 696320 | tf_op jit(solution)/shard_map/all_gather | solution.py:72
  41.0 0.0 copy-done.3
  41.0 15.7 %all_gather.7 = bf16[640,320]{0,1:T(8,128)(2,1)S(1)} all-gather(bf16[640,80]{0,1:T(8,128)(2,1)S(1)} %copy-done.3), channel_id=1, replica_groups=mesh['y_hi'=2,'z'=16,'core'=2,'x'=4,'y_lo'=2] {'y_hi','core'}, dimensions={1}, use_global_device_ids=true | all-gather | bytes 512000 | tf_op jit(solution)/shard_map/all_gather | solution.py:70
  56.8 0.4 convolution_convert_fusion
  57.2 0.2 copy.27
  57.4 0.3 reshape.147
  57.8 0.0 copy-start.1
  57.8 1.1 %copy.28 = bf16[4,8,16,4,80]{4,2,3,1,0:T(8,128)(2,1)} copy(bf16[4,8,16,4,80]{4,0,3,1,2:T(4,128)(2,1)S(1)} %bitcast.33) | data formatting | bytes 655360 | tf_op jit(solution)/shard_map/transpose | solution.py:75
  58.9 6.7 %all-to-all-start = ((bf16[32,16,4,80]{3,1,2,0:T(8,128)(2,1)}), bf16[32,16,4,80]{3,1,2,0:T(8,128)(2,1)S(1)}, u32[]{:S(2)}, u32[]{:S(2)}) async-start(bf16[32,16,4,80]{3,1,2,0:T(8,128)(2,1)} %bitcast.4), calls=%async_computation | async-start | bytes 1048576 | tf_op jit(solution)/shard_map/all_to_all | solution.py:76
  65.7 0.1 compare_select_fusion
  65.7 0.1 reshape.153
  65.8 0.0 copy-done.1
  65.8 0.0 copy-start.4
  65.8 0.0 copy-start.7
  65.8 1.9 %gather_fusion = s32[256]{0:T(256)S(1)} fusion(s32[128]{0:T(128)S(1)} %copy-done.1, s32[1024]{0:T(1024)S(1)} %pad_clamp_fusion.1), kind=kCustom, calls=%fused_computation | custom fusion | bytes 3072 | tf_op jit(solution)/shard_map/gather | solution.py:85
  67.7 0.1 reshape.152
  67.8 9.0 %all-to-all-done = bf16[32,16,4,80]{3,1,2,0:T(8,128)(2,1)S(1)} async-done(((bf16[32,16,4,80]{3,1,2,0:T(8,128)(2,1)}), bf16[32,16,4,80]{3,1,2,0:T(8,128)(2,1)S(1)}, u32[]{:S(2)}, u32[]{:S(2)}) %all-to-all-start) | async-done | bytes 327712 | tf_op jit(solution)/shard_map/all_to_all | solution.py:76
  76.8 0.1 convert_reduce_fusion
  76.9 0.1 copy.29
  77.0 0.0 copy-done.4
  77.0 0.0 copy-done.7
  77.0 0.9 %fusion.6 = bf16[4,64,80]{2,1,0:T(8,128)(2,1)} fusion(f32[4,64,80]{2,1,0:T(8,128)S(1)} %bitcast.35, bf16[4,64,80]{2,1,0:T(8,128)(2,1)S(1)} %copy-done.4, s32[4,64]{1,0:T(4,128)S(1)} %reshape.152, f32[50,80]{1,0:T(8,128)S(1)} %copy-done.7), kind=kOutput, calls=%fused_computation.12 | convolution fusion | flops 12382720 | bytes 180864 | tf_op jit(solution)/shard_map/tgs,sc->tgc/dot_general | solution.py:89
  (9 shorter events, 0.1 us)
Async XLA Ops:
  0.0 1.7 %copy-start = (bf16[16,16,640]{2,1,0:T(8,128)(2,1)S(1)}, bf16[16,16,640]{2,1,0:T(8,128)(2,1)}, u32[]{:S(2)}) copy-start(bf16[16,16,640]{2,1,0:T(8,128)(2,1)} %param.15) | copy-start | bytes 983044
  3.1 0.8 %copy-start.5 = (bf16[32,640]{1,0:T(8,128)(2,1)S(1)}, bf16[32,640]{1,0:T(8,128)(2,1)}, u32[]{:S(2)}) copy-start(bf16[32,640]{1,0:T(8,128)(2,1)} %param.12) | copy-start | bytes 122884
  3.1 1.0 %copy-start.2 = (bf16[16,16,640]{2,1,0:T(8,128)(2,1)S(1)}, bf16[16,16,640]{2,1,0:T(8,128)(2,1)}, u32[]{:S(2)}) copy-start(bf16[16,16,640]{2,1,0:T(8,128)(2,1)} %param.14) | copy-start | bytes 983044
  5.5 0.8 %copy-start.6 = (bf16[32,640]{1,0:T(8,128)(2,1)S(1)}, bf16[32,640]{1,0:T(8,128)(2,1)}, u32[]{:S(2)}) copy-start(bf16[32,640]{1,0:T(8,128)(2,1)} %param.11) | copy-start | bytes 122884
  5.5 0.8 %copy-start.8 = (s32[2]{0:T(128)S(1)}, s32[2]{0:T(128)}, u32[]{:S(2)}) copy-start(s32[2]{0:T(128)} %param.17) | copy-start | bytes 28
  6.9 34.1 %copy-start.3 = (bf16[640,80]{0,1:T(8,128)(2,1)S(1)}, bf16[640,80]{0,1:T(8,128)(2,1)}, u32[]{:S(2)}) copy-start(bf16[640,80]{0,1:T(8,128)(2,1)} %param.20) | copy-start | bytes 307204
  57.8 8.1 %copy-start.1 = (s32[128]{0:T(128)S(1)}, s32[128]{0:T(128)}, u32[]{:S(2)}) copy-start(s32[128]{0:T(128)} %param.18) | copy-start | bytes 1540
  58.9 17.9 %all-to-all-start = ((bf16[32,16,4,80]{3,1,2,0:T(8,128)(2,1)}), bf16[32,16,4,80]{3,1,2,0:T(8,128)(2,1)S(1)}, u32[]{:S(2)}, u32[]{:S(2)}) async-start(bf16[32,16,4,80]{3,1,2,0:T(8,128)(2,1)} %bitcast.4), calls=%async_computation | async-start | bytes 1048576 | tf_op jit(solution)/shard_map/all_to_all | solution.py:76
  65.8 11.2 %copy-start.4 = (bf16[4,64,80]{2,1,0:T(8,128)(2,1)S(1)}, bf16[4,64,80]{2,1,0:T(8,128)(2,1)}, u32[]{:S(2)}) copy-start(bf16[4,64,80]{2,1,0:T(8,128)(2,1)} %param.21) | copy-start | bytes 122884
  65.8 11.2 %copy-start.7 = (f32[50,80]{1,0:T(8,128)S(1)}, f32[50,80]{1,0:T(8,128)}, u32[]{:S(2)}) copy-start(f32[50,80]{1,0:T(8,128)} %param.19) | copy-start | bytes 48004

commit v2 on v1

v2 whole, which is shorter than its diff:
```python
import math

import jax
import jax.numpy as jnp
from jax import lax
from jax.experimental import pallas as pl
from jax.experimental.pallas import tpu as pltpu
from jax.sharding import Mesh
from jax.sharding import PartitionSpec as P

HEAD = 128
HIDDEN = -1e30


def nt_dot(left, right):
    return lax.dot_general(left, right, (((1,), (1,)), ((), ())), preferred_element_type=jnp.float32)


def attend_kernel(table, lengths, query, new_key, new_value, key_pool, value_pool, out):
    req_dev, pages = table.shape
    tok_count, width = query.shape
    cached = key_pool.shape[0]
    page_len = cached // pages
    new_count = tok_count // req_dev
    slot = lax.broadcasted_iota(jnp.int32, (1, cached), 1)
    page = slot // page_len
    inner = slot - page * page_len
    row_req = lax.broadcasted_iota(jnp.int32, (tok_count, 1), 0) // new_count
    seen = jnp.zeros((tok_count, cached), jnp.int32)
    for req in range(req_dev):
        left = jnp.zeros((1, cached), jnp.int32)
        for entry in range(pages):
            left = jnp.where(
                page == table[req, entry], jnp.maximum(left, lengths[req] - entry * page_len), left
            )
        seen = jnp.where(row_req == req, (inner < left).astype(jnp.int32), seen)
    new_req = lax.broadcasted_iota(jnp.int32, (1, tok_count), 1) // new_count
    own = row_req == new_req
    pool_seen = seen > 0
    scale = 1.0 / math.sqrt(HEAD)
    for head in range(width // HEAD):
        at = slice(head * HEAD, (head + 1) * HEAD)
        q = query[:, at]
        pool_score = jnp.where(pool_seen, nt_dot(q, key_pool[:, at]) * scale, HIDDEN)
        new_score = jnp.where(own, nt_dot(q, new_key[:, at]) * scale, HIDDEN)
        top = jnp.maximum(
            jnp.max(pool_score, axis=1, keepdims=True), jnp.max(new_score, axis=1, keepdims=True)
        )
        pool_exp = jnp.exp(pool_score - top)
        new_exp = jnp.exp(new_score - top)
        total = jnp.sum(pool_exp, axis=1, keepdims=True) + jnp.sum(new_exp, axis=1, keepdims=True)
        mixed = jnp.dot(
            (pool_exp / total).astype(jnp.bfloat16),
            value_pool[:, at],
            preferred_element_type=jnp.float32,
        ) + jnp.dot(
            (new_exp / total).astype(jnp.bfloat16),
            new_value[:, at],
            preferred_element_type=jnp.float32,
        )
        out[:, at] = mixed.astype(jnp.bfloat16)


def attend(queries, new_keys, new_values, key_pool, value_pool, page_table, lengths, interpret=False):
    smem = pl.BlockSpec(memory_space=pltpu.SMEM)
    vmem = pl.BlockSpec(memory_space=pltpu.VMEM)
    width = queries.shape[1]
    return pl.pallas_call(
        attend_kernel,
        out_shape=jax.ShapeDtypeStruct(queries.shape, jnp.bfloat16),
        in_specs=[smem, smem] + [vmem] * 5,
        out_specs=vmem,
        interpret=interpret,
        name="attend",
    )(
        page_table,
        lengths,
        queries,
        new_keys,
        new_values,
        key_pool.reshape(-1, width),
        value_pool.reshape(-1, width),
    )


def per_device(
    queries,
    new_keys,
    new_values,
    key_pool,
    value_pool,
    page_table,
    lengths,
    timesteps,
    gate_table,
    out_weight,
    residual,
):
    req_dev = page_table.shape[0]
    group_tok = queries.shape[0]
    new_count = group_tok // req_dev
    share = residual.shape[0]
    groups = residual.shape[1]
    col_count = out_weight.shape[1]
    y_hi, z_len, cores = (lax.axis_size(name) for name in ("y_hi", "z", "core"))
    tensor_len = lax.axis_size("x") * lax.axis_size("y_lo")
    own_columns = jnp.broadcast_to(out_weight.T[None], (y_hi * cores, col_count, out_weight.shape[0]))
    weight = lax.all_to_all(own_columns, ("y_hi", "core"), 0, 0, tiled=True)
    weight = weight.reshape(-1, out_weight.shape[0])
    attn = attend(queries, new_keys, new_values, key_pool, value_pool, page_table, lengths)
    attn_all = lax.all_gather(attn, "z", axis=0, tiled=True)
    partial = nt_dot(attn_all, weight).astype(jnp.bfloat16)
    blocks = partial.reshape(z_len, tensor_len, share, y_hi * cores, col_count)
    blocks = blocks.transpose(3, 1, 0, 2, 4).reshape(-1, z_len, share, col_count)
    arrived = lax.all_to_all(blocks, ("y_hi", "core", "x", "y_lo"), 0, 0, tiled=True)
    arrived = arrived.reshape(y_hi, cores, tensor_len, z_len, share, col_count)
    branch = jnp.sum(arrived.astype(jnp.float32), axis=2)
    branch = branch.transpose(3, 0, 2, 1, 4).reshape(share, groups, col_count)
    tensor_at = lax.axis_index(("x", "y_lo"))
    local_rows = tensor_at * share + jnp.arange(share, dtype=jnp.int32)
    request_at = (
        jnp.arange(groups, dtype=jnp.int32)[None, :] * req_dev + (local_rows // new_count)[:, None]
    )
    step_at = timesteps[request_at]
    onehot = (
        step_at[:, :, None] == jnp.arange(gate_table.shape[0], dtype=jnp.int32)[None, None, :]
    ).astype(jnp.float32)
    gate = jnp.einsum("tgs,sc->tgc", onehot, gate_table, precision=lax.Precision.HIGHEST)
    return (residual.astype(jnp.float32) + gate * branch).astype(jnp.bfloat16)


def solution(mesh):
    dp = ("y_hi", "z", "core")
    tensor = ("x", "y_lo")
    split = Mesh(mesh.devices.reshape(2, -1, 2, 4, 2), dp + tensor)
    placed = (
        P(dp, tensor),
        P(dp, tensor),
        P(dp, tensor),
        P(dp, None, tensor),
        P(dp, None, tensor),
        P(dp, None),
        P(dp),
        P(),
        P(None, dp),
        P(tensor, dp),
        P(tensor, None, dp),
    )
    return jax.shard_map(
        per_device, mesh=split, in_specs=placed, out_specs=P(tensor, None, dp), check_vma=False
    )
```

time: 78.3 us -> 73.6 us (0.940)
  blocking collectives: 49.2 us -> 27.7 us
  starting transfers between devices: 6.7 us -> 25 us
  Pallas kernels: 0 us -> 3.64 us
  local copies, waits for them, and re-layouts: 9.43 us -> 6.21 us
  matrix products: 2.43 us -> 1.38 us
    all_gather x1 -> x0, blocking collectives: 15.7 us -> none  [per_device(): weight = lax.all_gather(out_weight, ('y_hi', 'core'), axis=1, tiled=True)]
    all_to_all x0 -> x1, starting transfers between devices: none -> 10.3 us  [per_device(): weight = lax.all_to_all(own_columns, ('y_hi', 'core'), 0, 0, tiled=True)]
    all_to_all x1, starting transfers between devices: 6.7 us -> 14.7 us  [per_device(): lax.all_to_all(blocks, ('y_hi', 'core', 'x', 'y_lo'), 0, 0, tiled=True)]
    all_gather x1, blocking collectives: 33.5 us -> 27.7 us  [per_device(): attn_all = lax.all_gather(attn, 'z', axis=0, tiled=True)]
    pallas_call x0 -> x1, Pallas kernels: none -> 3.64 us  [attend(): pl.pallas_call(attend_kernel, out_shape=jax.ShapeDtypeStruct(queries.shap...]
    concatenate x8 -> x0, local copies, waits for them, and re-layouts: 2.63 us -> none  [the longest x4 1.73 us: attend(): jnp.concatenate([value_pool[page_table].reshape(req_dev, cached, width),...]
    broadcast_in_dim x1, local copies, waits for them, and re-layouts: 0.08 us -> 1.68 us  [per_device(): jnp.broadcast_to(out_weight.T[None], (y_hi * cores, col_count, out_weight...]
    gather x2 -> x0, local copies, waits for them, and re-layouts: 1.33 us -> none  [the longest x1 0.67 us: attend(): value_pool[page_table].reshape(req_dev, cached, width)]
  transfers between devices with their start and end apart: 1 -> 2, of which waited for: 1 -> 1; matrix products, arithmetic and copies ran while one was open for 3% -> 3% of each run, Pallas kernels for 0% -> 5%
where the time goes in v2:
time: 73.6 us; the launch traced here: 73.3 us
  blocking collectives  27.7 us (38%)
  starting transfers between devices  25 us (34%)
  waiting for transfers between devices  9.06 us (12%)
  local copies, waits for them, and re-layouts  6.21 us (8%)
  Pallas kernels  3.64 us (5%)
  matrix products  1.38 us (2%)
    all_gather x1, blocking collectives, per_device(): attn_all = lax.all_gather(attn, 'z', axis=0, tiled=True)  27.7 us
    all_to_all x1, starting transfers between devices, per_device(): lax.all_to_all(blocks, ('y_hi', 'core', 'x', 'y_lo'), 0, 0, tiled=True)  14.7 us
    all_to_all x1, starting transfers between devices, per_device(): weight = lax.all_to_all(own_columns, ('y_hi', 'core'), 0, 0, tiled=True)  10.3 us
    all_to_all x1, waiting for transfers between devices, per_device(): lax.all_to_all(blocks, ('y_hi', 'core', 'x', 'y_lo'), 0, 0, tiled=True)  9.06 us
    pallas_call x1, Pallas kernels, attend(): pl.pallas_call(attend_kernel, out_shape=jax.ShapeDtypeStruct(queries.shap...  3.64 us
    gather x2, local copies, waits for them, and re-layouts, per_device(): step_at = timesteps[request_at]  1.95 us
    broadcast_in_dim x1, local copies, waits for them, and re-layouts, per_device(): jnp.broadcast_to(out_weight.T[None], (y_hi * cores, col_count, out_weight...  1.68 us
  transfers between devices with their start and end apart: 2, of which 1 were waited for; matrix products, arithmetic and copies ran while one was open for 3% of the time, Pallas kernels for 5%

profile of v2, /device:TPU:1, one launch (start us, length us, event | category | flops | bytes accessed | tf_op | source)
XLA Modules:
  0.0 73.3 jit_solution(15092460213941559054)
XLA Ops:
  0.0 0.0 copy-start
  0.0 1.7 %broadcast_in_dim.2 = bf16[4,80,640]{2,1,0:T(8,128)(2,1)} broadcast(bf16[80,640]{1,0:T(8,128)(2,1)} %bitcast.24), dimensions={1,2} | broadcast | bytes 512000 | tf_op jit(solution)/shard_map/broadcast_in_dim | solution.py:107
  1.7 10.3 %all-to-all-start = ((bf16[4,80,640]{2,1,0:T(8,128)(2,1)}), bf16[4,80,640]{2,1,0:T(8,128)(2,1)S(1)}, u32[]{:S(2)}, u32[]{:S(2)}) async-start(bf16[4,80,640]{2,1,0:T(8,128)(2,1)} %broadcast_in_dim.2), calls=%async_computation | async-start | bytes 819200 | tf_op jit(solution)/shard_map/all_to_all | solution.py:108
  12.0 3.6 %attend.1 = bf16[32,640]{1,0:T(8,128)(2,1)} custom-call(s32[2,16]{1,0:T(2,128)} %table.1, s32[2]{0:T(128)} %lengths.1, bf16[32,640]{1,0:T(8,128)(2,1)} %query.1, bf16[32,640]{1,0:T(8,128)(2,1)} %new_key.1, bf16[32,640]{1,0:T(8,128)(2,1)} %new_value.1, bf16[256,640]{1,0:T(8,128)(2,1)} %bitcast.22, bf16[256,640]{1,0:T(8,128)(2,1)} %bitcast.23), custom_call_target="tpu_custom_call" | custom-call | tf_op jit(solution)/shard_map/attend/pallas_call | solution.py:68
  15.6 27.7 %all_gather.3 = bf16[512,640]{1,0:T(8,128)(2,1)S(1)} all-gather(bf16[32,640]{1,0:T(8,128)(2,1)} %attend.1), channel_id=1, replica_groups=mesh['y_hi'=2,'z'=16,'core'=2,'x'=4,'y_lo'=2] {'z'}, dimensions={0}, use_global_device_ids=true | all-gather | bytes 696320 | tf_op jit(solution)/shard_map/all_gather | solution.py:111
  43.3 0.0 all-to-all-done
  43.3 0.4 convolution_convert_fusion
  43.8 0.2 copy.14
  44.0 0.3 reshape.102
  44.3 1.1 %copy.15 = bf16[4,8,16,4,80]{4,2,3,1,0:T(8,128)(2,1)} copy(bf16[4,8,16,4,80]{4,0,3,1,2:T(4,128)(2,1)S(1)} %bitcast.18) | data formatting | bytes 655360 | tf_op jit(solution)/shard_map/transpose | solution.py:114
  45.5 0.0 copy-start.1
  45.5 14.7 %all-to-all-start.1 = ((bf16[32,16,4,80]{3,1,2,0:T(8,128)(2,1)}), bf16[32,16,4,80]{3,1,2,0:T(8,128)(2,1)S(1)}, u32[]{:S(2)}, u32[]{:S(2)}) async-start(bf16[32,16,4,80]{3,1,2,0:T(8,128)(2,1)} %bitcast.6), calls=%async_computation.1 | async-start | bytes 1048576 | tf_op jit(solution)/shard_map/all_to_all | solution.py:115
  60.2 0.1 compare_select_fusion
  60.3 0.1 reshape.108
  60.4 0.0 copy-done.1
  60.4 1.9 %gather_fusion = s32[256]{0:T(256)S(1)} fusion(s32[128]{0:T(128)S(1)} %copy-done.1, s32[1024]{0:T(1024)S(1)} %pad_clamp_fusion), kind=kCustom, calls=%fused_computation | custom fusion | bytes 3072 | tf_op jit(solution)/shard_map/gather | solution.py:124
  62.3 0.1 reshape.107
  62.3 9.1 %all-to-all-done.1 = bf16[32,16,4,80]{3,1,2,0:T(8,128)(2,1)S(1)} async-done(((bf16[32,16,4,80]{3,1,2,0:T(8,128)(2,1)}), bf16[32,16,4,80]{3,1,2,0:T(8,128)(2,1)S(1)}, u32[]{:S(2)}, u32[]{:S(2)}) %all-to-all-start.1) | async-done | bytes 327712 | tf_op jit(solution)/shard_map/all_to_all | solution.py:115
  71.4 0.1 convert_reduce_fusion
  71.5 0.0 copy-start.2
  71.5 0.1 copy.16
  71.6 0.0 copy-done
  71.6 0.7 copy-done.2
  72.4 0.9 %fusion.1 = bf16[4,64,80]{2,1,0:T(8,128)(2,1)} fusion(f32[4,64,80]{2,1,0:T(8,128)S(1)} %bitcast.21, bf16[4,64,80]{2,1,0:T(8,128)(2,1)S(1)} %copy-done.2, s32[4,64]{1,0:T(4,128)S(1)} %reshape.107, f32[50,80]{1,0:T(8,128)S(1)} %copy-done), kind=kOutput, calls=%fused_computation.4 | convolution fusion | flops 12382720 | bytes 180864 | tf_op jit(solution)/shard_map/tgs,sc->tgc/dot_general | solution.py:128
  (3 shorter events, 0.0 us)
Async XLA Ops:
  0.0 71.6 %copy-start = (f32[50,80]{1,0:T(8,128)S(1)}, f32[50,80]{1,0:T(8,128)}, u32[]{:S(2)}) copy-start(f32[50,80]{1,0:T(8,128)} %param.19) | copy-start | bytes 48004
  1.7 41.6 %all-to-all-start = ((bf16[4,80,640]{2,1,0:T(8,128)(2,1)}), bf16[4,80,640]{2,1,0:T(8,128)(2,1)S(1)}, u32[]{:S(2)}, u32[]{:S(2)}) async-start(bf16[4,80,640]{2,1,0:T(8,128)(2,1)} %broadcast_in_dim.2), calls=%async_computation | async-start | bytes 819200 | tf_op jit(solution)/shard_map/all_to_all | solution.py:108
  45.5 14.9 %copy-start.1 = (s32[128]{0:T(128)S(1)}, s32[128]{0:T(128)}, u32[]{:S(2)}) copy-start(s32[128]{0:T(128)} %param.18) | copy-start | bytes 1540
  45.5 25.9 %all-to-all-start.1 = ((bf16[32,16,4,80]{3,1,2,0:T(8,128)(2,1)}), bf16[32,16,4,80]{3,1,2,0:T(8,128)(2,1)S(1)}, u32[]{:S(2)}, u32[]{:S(2)}) async-start(bf16[32,16,4,80]{3,1,2,0:T(8,128)(2,1)} %bitcast.6), calls=%async_computation.1 | async-start | bytes 1048576 | tf_op jit(solution)/shard_map/all_to_all | solution.py:115
  71.5 0.8 %copy-start.2 = (bf16[4,64,80]{2,1,0:T(8,128)(2,1)S(1)}, bf16[4,64,80]{2,1,0:T(8,128)(2,1)}, u32[]{:S(2)}) copy-start(bf16[4,64,80]{2,1,0:T(8,128)(2,1)} %param.21) | copy-start | bytes 122884

commit v3 on v2

--- a/solution.py
+++ b/solution.py
@@ -83,6 +83,79 @@
     )
 
 
+def project_kernel(attn, weight, out, packed):
+    blocks, tensor_len, rows, lanes = out.shape
+    cols = weight.shape[0] // blocks
+    half = attn.shape[0] // 2
+    share = half // (tensor_len * rows)
+    to = lax.broadcasted_iota(jnp.int32, (half, half), 0)
+    source = (
+        (to % rows) * (tensor_len * share)
+        + (to // rows) % tensor_len * share
+        + to // (rows * tensor_len)
+    )
+    order = (source == lax.broadcasted_iota(jnp.int32, (half, half), 1)).astype(jnp.bfloat16)
+    sorted_rows = [
+        jnp.dot(
+            order, attn[part * half : (part + 1) * half, :], preferred_element_type=jnp.float32
+        ).astype(jnp.bfloat16)
+        for part in range(2)
+    ]
+    run = tensor_len * rows
+    for block in range(blocks):
+        block_weight = weight[block * cols : (block + 1) * cols, :]
+        for part in range(2):
+            partial = nt_dot(sorted_rows[part], block_weight)
+            for row in range(share):
+                at = (part * share + row) * cols
+                packed[:, at : at + cols] = partial[row * run : (row + 1) * run]
+        out[block] = packed[...].astype(jnp.bfloat16).reshape(tensor_len, rows, lanes)
+
+
+def project(attn, weight, blocks, tensor_len, interpret=False):
+    cols = weight.shape[0] // blocks
+    rows = 8
+    lanes = attn.shape[0] // (tensor_len * rows) * cols
+    vmem = pl.BlockSpec(memory_space=pltpu.VMEM)
+    return pl.pallas_call(
+        project_kernel,
+        out_shape=jax.ShapeDtypeStruct((blocks, tensor_len, rows, lanes), jnp.bfloat16),
+        in_specs=[vmem, vmem],
+        out_specs=vmem,
+        scratch_shapes=[pltpu.VMEM((tensor_len * rows, lanes), jnp.float32)],
+        interpret=interpret,
+        name="project",
+    )(attn, weight)
+
+
+def finish_kernel(arrived, gate, residual, out, branch):
+    y_hi, cores, tensor_len, rows, lanes = arrived.shape
+    share, groups, cols = residual.shape
+    for side in range(y_hi):
+        for core in range(cores):
+            total = jnp.sum(arrived[side, core].astype(jnp.float32), axis=0)
+            for place in range(lanes // cols):
+                first = (side * (groups // y_hi)) + (place // share) * rows * cores + core
+                branch[place % share, pl.ds(first, rows, cores), :] = total[
+                    :, place * cols : (place + 1) * cols
+                ]
+    for row in range(share):
+        out[row] = (residual[row].astype(jnp.float32) + gate[...] * branch[row]).astype(jnp.bfloat16)
+
+
+def finish(arrived, gate, residual, interpret=False):
+    vmem = pl.BlockSpec(memory_space=pltpu.VMEM)
+    return pl.pallas_call(
+        finish_kernel,
+        out_shape=jax.ShapeDtypeStruct(residual.shape, residual.dtype),
+        in_specs=[vmem, vmem, vmem],
+        out_specs=vmem,
+        scratch_shapes=[pltpu.VMEM(residual.shape, jnp.float32)],
+        interpret=interpret,
+        name="finish",
+    )(arrived, gate, residual)
+
+
 def per_device(
     queries,
     new_keys,
@@ -102,31 +175,23 @@
     share = residual.shape[0]
     groups = residual.shape[1]
     col_count = out_weight.shape[1]
-    y_hi, z_len, cores = (lax.axis_size(name) for name in ("y_hi", "z", "core"))
+    y_hi, cores = (lax.axis_size(name) for name in ("y_hi", "core"))
     tensor_len = lax.axis_size("x") * lax.axis_size("y_lo")
     own_columns = jnp.broadcast_to(out_weight.T[None], (y_hi * cores, col_count, out_weight.shape[0]))
     weight = lax.all_to_all(own_columns, ("y_hi", "core"), 0, 0, tiled=True)
     weight = weight.reshape(-1, out_weight.shape[0])
     attn = attend(queries, new_keys, new_values, key_pool, value_pool, page_table, lengths)
     attn_all = lax.all_gather(attn, "z", axis=0, tiled=True)
-    partial = nt_dot(attn_all, weight).astype(jnp.bfloat16)
-    blocks = partial.reshape(z_len, tensor_len, share, y_hi * cores, col_count)
-    blocks = blocks.transpose(3, 1, 0, 2, 4).reshape(-1, z_len, share, col_count)
+    blocks = project(attn_all, weight, y_hi * cores, tensor_len)
+    blocks = blocks.reshape(-1, *blocks.shape[2:])
     arrived = lax.all_to_all(blocks, ("y_hi", "core", "x", "y_lo"), 0, 0, tiled=True)
-    arrived = arrived.reshape(y_hi, cores, tensor_len, z_len, share, col_count)
-    branch = jnp.sum(arrived.astype(jnp.float32), axis=2)
-    branch = branch.transpose(3, 0, 2, 1, 4).reshape(share, groups, col_count)
-    tensor_at = lax.axis_index(("x", "y_lo"))
-    local_rows = tensor_at * share + jnp.arange(share, dtype=jnp.int32)
-    request_at = (
-        jnp.arange(groups, dtype=jnp.int32)[None, :] * req_dev + (local_rows // new_count)[:, None]
-    )
-    step_at = timesteps[request_at]
-    onehot = (
-        step_at[:, :, None] == jnp.arange(gate_table.shape[0], dtype=jnp.int32)[None, None, :]
-    ).astype(jnp.float32)
-    gate = jnp.einsum("tgs,sc->tgc", onehot, gate_table, precision=lax.Precision.HIGHEST)
-    return (residual.astype(jnp.float32) + gate * branch).astype(jnp.bfloat16)
+    request_at = lax.axis_index(("x", "y_lo")) * share // new_count
+    step_at = lax.dynamic_index_in_dim(timesteps.reshape(groups, req_dev), request_at, 1, False)
+    onehot = (step_at[:, None] == jnp.arange(gate_table.shape[0], dtype=jnp.int32)[None, :]).astype(
+        jnp.float32
+    )
+    gate = jnp.dot(onehot, gate_table, precision=lax.Precision.HIGHEST)
+    return finish(arrived.reshape(y_hi, cores, tensor_len, *arrived.shape[1:]), gate, residual)
 
 
 def solution(mesh):

time: 73.6 us -> 76.4 us (1.038)
  Pallas kernels: 3.64 us -> 8.55 us
  blocking collectives: 27.7 us -> 30.4 us
  local copies, waits for them, and re-layouts: 6.21 us -> 4.12 us
  waiting for transfers between devices: 9.06 us -> 7.45 us
    pallas_call x0 -> x2, Pallas kernels: none -> 4.92 us  [the longest x1 3.16 us: project(): pl.pallas_call(project_kernel, out_shape=jax.ShapeDtypeStruct((blocks, te...]
    all_gather x1, blocking collectives: 27.7 us -> 30.4 us  [per_device(): attn_all = lax.all_gather(attn, 'z', axis=0, tiled=True)]
    gather x2 -> x0, local copies, waits for them, and re-layouts: 1.95 us -> none  [per_device(): step_at = timesteps[request_at]]
    all_to_all x1, waiting for transfers between devices: 9.06 us -> 7.44 us  [per_device(): lax.all_to_all(blocks, ('y_hi', 'core', 'x', 'y_lo'), 0, 0, tiled=True)]
    unnamed x6 -> x8, local copies, waits for them, and re-layouts: 0.72 us -> 2.13 us
    transpose x2 -> x0, local copies, waits for them, and re-layouts: 1.24 us -> none  [the longest x1 1.14 us: per_device(): blocks.transpose(3, 1, 0, 2, 4).reshape(-1, z_len, share, col_count)]
  transfers between devices with their start and end apart: 2 -> 2, of which waited for: 1 -> 1; matrix products, arithmetic and copies ran while one was open for 3% -> 1% of each run, Pallas kernels for 5% -> 5%
where the time goes in v3:
time: 76.4 us; the launch traced here: 76.1 us
  blocking collectives  30.4 us (40%)
  starting transfers between devices  24.6 us (32%)
  Pallas kernels  8.55 us (11%)
  waiting for transfers between devices  7.45 us (10%)
  local copies, waits for them, and re-layouts  4.12 us (5%)
  matrix products  0.81 us (1%)
    all_gather x1, blocking collectives, per_device(): attn_all = lax.all_gather(attn, 'z', axis=0, tiled=True)  30.4 us
    all_to_all x1, starting transfers between devices, per_device(): lax.all_to_all(blocks, ('y_hi', 'core', 'x', 'y_lo'), 0, 0, tiled=True)  14.4 us
    all_to_all x1, starting transfers between devices, per_device(): weight = lax.all_to_all(own_columns, ('y_hi', 'core'), 0, 0, tiled=True)  10.3 us
    all_to_all x1, waiting for transfers between devices, per_device(): lax.all_to_all(blocks, ('y_hi', 'core', 'x', 'y_lo'), 0, 0, tiled=True)  7.44 us
    pallas_call x1, Pallas kernels, attend(): pl.pallas_call(attend_kernel, out_shape=jax.ShapeDtypeStruct(queries.shap...  3.63 us
    pallas_call x1, Pallas kernels, project(): pl.pallas_call(project_kernel, out_shape=jax.ShapeDtypeStruct((blocks, te...  3.16 us
    unnamed x8, local copies, waits for them, and re-layouts  2.13 us
    pallas_call x1, Pallas kernels, finish(): pl.pallas_call(finish_kernel, out_shape=jax.ShapeDtypeStruct(residual.sha...  1.77 us
  transfers between devices with their start and end apart: 2, of which 1 were waited for; matrix products, arithmetic and copies ran while one was open for 1% of the time, Pallas kernels for 5%

profile of v3, /device:TPU:1, one launch (start us, length us, event | category | flops | bytes accessed | tf_op | source)
XLA Modules:
  0.0 76.1 jit_solution(7771727537016981582)
XLA Ops:
  0.0 0.0 copy-start
  0.0 1.7 %broadcast_in_dim.2 = bf16[4,80,640]{2,1,0:T(8,128)(2,1)} broadcast(bf16[80,640]{1,0:T(8,128)(2,1)} %bitcast.12), dimensions={1,2} | broadcast | bytes 512000 | tf_op jit(solution)/shard_map/broadcast_in_dim | solution.py:180
  1.7 10.3 %all-to-all-start = ((bf16[4,80,640]{2,1,0:T(8,128)(2,1)}), bf16[4,80,640]{2,1,0:T(8,128)(2,1)S(1)}, u32[]{:S(2)}, u32[]{:S(2)}) async-start(bf16[4,80,640]{2,1,0:T(8,128)(2,1)} %broadcast_in_dim.2), calls=%async_computation | async-start | bytes 819200 | tf_op jit(solution)/shard_map/all_to_all | solution.py:181
  12.0 3.6 %attend.1 = bf16[32,640]{1,0:T(8,128)(2,1)} custom-call(s32[2,16]{1,0:T(2,128)} %table.1, s32[2]{0:T(128)} %lengths.1, bf16[32,640]{1,0:T(8,128)(2,1)} %query.1, bf16[32,640]{1,0:T(8,128)(2,1)} %new_key.1, bf16[32,640]{1,0:T(8,128)(2,1)} %new_value.1, bf16[256,640]{1,0:T(8,128)(2,1)} %bitcast.10, bf16[256,640]{1,0:T(8,128)(2,1)} %bitcast.11), custom_call_target="tpu_custom_call" | custom-call | tf_op jit(solution)/shard_map/attend/pallas_call | solution.py:68
  15.6 30.4 %all_gather.3.attn = bf16[512,640]{1,0:T(8,128)(2,1)} all-gather(bf16[32,640]{1,0:T(8,128)(2,1)} %attend.1), channel_id=1, replica_groups=mesh['y_hi'=2,'z'=16,'core'=2,'x'=4,'y_lo'=2] {'z'}, dimensions={0}, use_global_device_ids=true | all-gather | bytes 696320 | tf_op jit(solution)/shard_map/all_gather | solution.py:184
  46.0 0.0 all-to-all-done
  46.0 0.0 copy-start.1
  46.0 0.8 copy-done.1
  46.8 3.2 %project.1 = bf16[4,8,8,640]{3,2,1,0:T(8,128)(2,1)} custom-call(bf16[512,640]{1,0:T(8,128)(2,1)} %all_gather.3.attn, bf16[320,640]{1,0:T(8,128)(2,1)} %bitcast.7), custom_call_target="tpu_custom_call" | custom-call | tf_op jit(solution)/shard_map/project/pallas_call | solution.py:120
  49.9 14.4 %all-to-all-start.1 = ((bf16[32,8,640]{2,1,0:T(8,128)(2,1)}), bf16[32,8,640]{2,1,0:T(8,128)(2,1)S(1)}, u32[]{:S(2)}, u32[]{:S(2)}) async-start(bf16[32,8,640]{2,1,0:T(8,128)(2,1)} %bitcast.9), calls=%async_computation.1 | async-start | bytes 655360 | tf_op jit(solution)/shard_map/all_to_all | solution.py:187
  64.3 0.0 copy-start.3
  64.3 0.6 copy-done.3
  65.0 0.1 reshape.24
  65.1 0.2 dynamic-slice_reduce_fusion
  65.3 0.0 copy-done
  65.3 0.8 %fusion.gate = f32[64,80]{1,0:T(8,128)} fusion(f32[50,80]{1,0:T(8,128)S(1)} %copy-done, s32[64]{0:T(128)S(1)} %dynamic-slice_reduce_fusion), kind=kOutput, calls=%fused_computation.2 | convolution fusion | flops 3075200 | bytes 36736 | tf_op jit(solution)/shard_map/dot_general | solution.py:193
  66.1 7.4 %all-to-all-done.1 = bf16[32,8,640]{2,1,0:T(8,128)(2,1)S(1)} async-done(((bf16[32,8,640]{2,1,0:T(8,128)(2,1)}), bf16[32,8,640]{2,1,0:T(8,128)(2,1)S(1)}, u32[]{:S(2)}, u32[]{:S(2)}) %all-to-all-start.1) | async-done | bytes 327712 | tf_op jit(solution)/shard_map/all_to_all | solution.py:187
  73.6 0.0 copy-start.2
  73.6 0.7 copy-done.2
  74.3 1.8 %finish.1 = bf16[4,64,80]{2,1,0:T(8,128)(2,1)} custom-call(bf16[2,2,8,8,640]{4,3,2,1,0:T(8,128)(2,1)} %bitcast.8, f32[64,80]{1,0:T(8,128)} %fusion.gate, bf16[4,64,80]{2,1,0:T(8,128)(2,1)} %residual.1), custom_call_target="tpu_custom_call" | custom-call | tf_op jit(solution)/shard_map/finish/pallas_call | solution.py:148
Async XLA Ops:
  0.0 65.3 %copy-start = (f32[50,80]{1,0:T(8,128)S(1)}, f32[50,80]{1,0:T(8,128)}, u32[]{:S(2)}) copy-start(f32[50,80]{1,0:T(8,128)} %param.19) | copy-start | bytes 48004
  1.7 44.3 %all-to-all-start = ((bf16[4,80,640]{2,1,0:T(8,128)(2,1)}), bf16[4,80,640]{2,1,0:T(8,128)(2,1)S(1)}, u32[]{:S(2)}, u32[]{:S(2)}) async-start(bf16[4,80,640]{2,1,0:T(8,128)(2,1)} %broadcast_in_dim.2), calls=%async_computation | async-start | bytes 819200 | tf_op jit(solution)/shard_map/all_to_all | solution.py:181
  46.0 0.8 copy-start.1
  49.9 23.6 %all-to-all-start.1 = ((bf16[32,8,640]{2,1,0:T(8,128)(2,1)}), bf16[32,8,640]{2,1,0:T(8,128)(2,1)S(1)}, u32[]{:S(2)}, u32[]{:S(2)}) async-start(bf16[32,8,640]{2,1,0:T(8,128)(2,1)} %bitcast.9), calls=%async_computation.1 | async-start | bytes 655360 | tf_op jit(solution)/shard_map/all_to_all | solution.py:187
  64.3 0.7 copy-start.3
  73.6 0.7 copy-start.2

commit v4 on v3

--- a/solution.py
+++ b/solution.py
@@ -10,6 +10,7 @@
 
 HEAD = 128
 HIDDEN = -1e30
+SMALL = pltpu.CompilerParams(vmem_limit_bytes=12 * 1024 * 1024)
 
 
 def nt_dot(left, right):
@@ -71,6 +72,7 @@
         in_specs=[smem, smem] + [vmem] * 5,
         out_specs=vmem,
         interpret=interpret,
+        compiler_params=SMALL,
         name="attend",
     )(
         page_table,
@@ -88,12 +90,12 @@
     cols = weight.shape[0] // blocks
     half = attn.shape[0] // 2
     share = half // (tensor_len * rows)
-    to = lax.broadcasted_iota(jnp.int32, (half, half), 0)
-    source = (
-        (to % rows) * (tensor_len * share)
-        + (to // rows) % tensor_len * share
-        + to // (rows * tensor_len)
-    )
+    to = lax.broadcasted_iota(jnp.int32, (half, 1), 0)
+    row_bits, tensor_bits = rows.bit_length() - 1, tensor_len.bit_length() - 1
+    row_at = to & (rows - 1)
+    tensor_at = (to >> row_bits) & (tensor_len - 1)
+    share_at = to >> (row_bits + tensor_bits)
+    source = (row_at * tensor_len + tensor_at) * share + share_at
     order = (source == lax.broadcasted_iota(jnp.int32, (half, half), 1)).astype(jnp.bfloat16)
     sorted_rows = [
         jnp.dot(
@@ -124,6 +126,7 @@
         out_specs=vmem,
         scratch_shapes=[pltpu.VMEM((tensor_len * rows, lanes), jnp.float32)],
         interpret=interpret,
+        compiler_params=SMALL,
         name="project",
     )(attn, weight)
 
@@ -152,6 +155,7 @@
         out_specs=vmem,
         scratch_shapes=[pltpu.VMEM(residual.shape, jnp.float32)],
         interpret=interpret,
+        compiler_params=SMALL,
         name="finish",
     )(arrived, gate, residual)
 

time: 76.4 us -> 69.6 us (0.911)
  Pallas kernels: 8.55 us -> 5.13 us
  blocking collectives: 30.4 us -> 28.1 us
  local copies, waits for them, and re-layouts: 4.12 us -> 3.3 us
    all_gather x1, blocking collectives: 30.4 us -> 28.1 us  [per_device(): attn_all = lax.all_gather(attn, 'z', axis=0, tiled=True)]
    pallas_call x1, Pallas kernels: 3.63 us -> 2.4 us  [attend(): pl.pallas_call(attend_kernel, out_shape=jax.ShapeDtypeStruct(queries.shap...]
    pallas_call x1, Pallas kernels: 3.16 us -> 1.96 us  [project(): pl.pallas_call(project_kernel, out_shape=jax.ShapeDtypeStruct((blocks, te...]
    pallas_call x1, Pallas kernels: 1.77 us -> 0.77 us  [finish(): pl.pallas_call(finish_kernel, out_shape=jax.ShapeDtypeStruct(residual.sha...]
    unnamed x8 -> x20, local copies, waits for them, and re-layouts: 2.13 us -> 1.32 us
  transfers between devices with their start and end apart: 2 -> 2, of which waited for: 1 -> 1; matrix products, arithmetic and copies ran while one was open for 1% -> 1% of each run, Pallas kernels for 5% -> 3%
where the time goes in v4:
time: 69.6 us; the launch traced here: 69.3 us
  blocking collectives  28.1 us (40%)
  starting transfers between devices  24.4 us (35%)
  waiting for transfers between devices  8.04 us (12%)
  Pallas kernels  5.13 us (7%)
  local copies, waits for them, and re-layouts  3.3 us (5%)
    all_gather x1, blocking collectives, per_device(): attn_all = lax.all_gather(attn, 'z', axis=0, tiled=True)  28.1 us
    all_to_all x1, starting transfers between devices, per_device(): lax.all_to_all(blocks, ('y_hi', 'core', 'x', 'y_lo'), 0, 0, tiled=True)  14 us
    all_to_all x1, starting transfers between devices, per_device(): weight = lax.all_to_all(own_columns, ('y_hi', 'core'), 0, 0, tiled=True)  10.4 us
    all_to_all x1, waiting for transfers between devices, per_device(): lax.all_to_all(blocks, ('y_hi', 'core', 'x', 'y_lo'), 0, 0, tiled=True)  8.04 us
    pallas_call x1, Pallas kernels, attend(): pl.pallas_call(attend_kernel, out_shape=jax.ShapeDtypeStruct(queries.shap...  2.4 us
    pallas_call x1, Pallas kernels, project(): pl.pallas_call(project_kernel, out_shape=jax.ShapeDtypeStruct((blocks, te...  1.96 us
    broadcast_in_dim x1, local copies, waits for them, and re-layouts, per_device(): jnp.broadcast_to(out_weight.T[None], (y_hi * cores, col_count, out_weight...  1.68 us
  transfers between devices with their start and end apart: 2, of which 1 were waited for; matrix products, arithmetic and copies ran while one was open for 1% of the time, Pallas kernels for 3%

profile of v4, /device:TPU:1, one launch (start us, length us, event | category | flops | bytes accessed | tf_op | source)
XLA Modules:
  0.0 69.3 jit_solution(10093688262268561781)
XLA Ops:
  0.0 0.0 copy-start
  0.0 1.7 %broadcast_in_dim.2 = bf16[4,80,640]{2,1,0:T(8,128)(2,1)} broadcast(bf16[80,640]{1,0:T(8,128)(2,1)} %bitcast.11), dimensions={1,2} | broadcast | bytes 512000 | tf_op jit(solution)/shard_map/broadcast_in_dim | solution.py:184
  1.7 0.0 copy-start.1
  1.7 0.0 copy-start.2
  1.7 0.0 copy-start.4
  1.7 0.0 copy-start.5
  1.7 0.0 copy-start.6
  1.7 10.4 %all-to-all-start = ((bf16[4,80,640]{2,1,0:T(8,128)(2,1)}), bf16[4,80,640]{2,1,0:T(8,128)(2,1)S(1)}, u32[]{:S(2)}, u32[]{:S(2)}) async-start(bf16[4,80,640]{2,1,0:T(8,128)(2,1)} %broadcast_in_dim.2), calls=%async_computation | async-start | bytes 819200 | tf_op jit(solution)/shard_map/all_to_all | solution.py:185
  12.1 0.0 copy-start.7
  12.1 0.0 copy-start.8
  12.1 0.0 copy-done.1
  12.1 0.0 copy-done.2
  12.1 0.0 copy-done.4
  12.1 0.0 copy-done.5
  12.1 0.0 copy-done.6
  12.2 0.6 copy-done.7
  12.8 0.0 copy-done.8
  12.8 2.4 %attend.1 = bf16[32,640]{1,0:T(8,128)(2,1)S(1)} custom-call(s32[2,16]{1,0:T(2,128)S(1)} %copy-done.7, s32[2]{0:T(128)S(1)} %copy-done.8, bf16[32,640]{1,0:T(8,128)(2,1)S(1)} %copy-done.4, bf16[32,640]{1,0:T(8,128)(2,1)S(1)} %copy-done.5, bf16[32,640]{1,0:T(8,128)(2,1)S(1)} %copy-done.6, bf16[256,640]{1,0:T(8,128)(2,1)S(1)} %bitcast.9, ...), custom_call_target="tpu_custom_call" | custom-call | tf_op jit(solution)/shard_map/attend/pallas_call | solution.py:69
  15.2 28.1 %all_gather.3.attn = bf16[512,640]{1,0:T(8,128)(2,1)S(1)} all-gather(bf16[32,640]{1,0:T(8,128)(2,1)S(1)} %attend.1), channel_id=1, replica_groups=mesh['y_hi'=2,'z'=16,'core'=2,'x'=4,'y_lo'=2] {'z'}, dimensions={0}, use_global_device_ids=true | all-gather | bytes 696320 | tf_op jit(solution)/shard_map/all_gather | solution.py:188
  43.3 0.0 all-to-all-done
  43.3 2.0 %project.1 = bf16[4,8,8,640]{3,2,1,0:T(8,128)(2,1)} custom-call(bf16[512,640]{1,0:T(8,128)(2,1)S(1)} %all_gather.3.attn, bf16[320,640]{1,0:T(8,128)(2,1)S(1)} %bitcast.7), custom_call_target="tpu_custom_call" | custom-call | tf_op jit(solution)/shard_map/project/pallas_call | solution.py:122
  45.2 14.0 %all-to-all-start.1 = ((bf16[32,8,640]{2,1,0:T(8,128)(2,1)}), bf16[32,8,640]{2,1,0:T(8,128)(2,1)S(1)}, u32[]{:S(2)}, u32[]{:S(2)}) async-start(bf16[32,8,640]{2,1,0:T(8,128)(2,1)} %bitcast.4), calls=%async_computation.1 | async-start | bytes 655360 | tf_op jit(solution)/shard_map/all_to_all | solution.py:191
  59.2 0.0 copy-start.9
  59.3 0.6 copy-done.9
  59.9 0.0 copy-start.3
  59.9 0.1 reshape.24
  60.0 0.2 dynamic-slice_reduce_fusion
  60.2 0.0 copy-done
  60.2 0.2 fusion.gate
  60.4 8.0 %all-to-all-done.1 = bf16[32,8,640]{2,1,0:T(8,128)(2,1)S(1)} async-done(((bf16[32,8,640]{2,1,0:T(8,128)(2,1)}), bf16[32,8,640]{2,1,0:T(8,128)(2,1)S(1)}, u32[]{:S(2)}, u32[]{:S(2)}) %all-to-all-start.1) | async-done | bytes 327712 | tf_op jit(solution)/shard_map/all_to_all | solution.py:191
  68.5 0.0 copy-done.3
  68.5 0.8 %finish.1 = bf16[4,64,80]{2,1,0:T(8,128)(2,1)} custom-call(bf16[2,2,8,8,640]{4,3,2,1,0:T(8,128)(2,1)S(1)} %bitcast.8, f32[64,80]{1,0:T(8,128)S(1)} %fusion.gate, bf16[4,64,80]{2,1,0:T(8,128)(2,1)S(1)} %copy-done.3), custom_call_target="tpu_custom_call" | custom-call | tf_op jit(solution)/shard_map/finish/pallas_call | solution.py:151
Async XLA Ops:
  0.0 60.2 %copy-start = (f32[50,80]{1,0:T(8,128)S(1)}, f32[50,80]{1,0:T(8,128)}, u32[]{:S(2)}) copy-start(f32[50,80]{1,0:T(8,128)} %param.19) | copy-start | bytes 48004
  1.7 10.4 %copy-start.1 = (bf16[16,16,640]{2,1,0:T(8,128)(2,1)S(1)}, bf16[16,16,640]{2,1,0:T(8,128)(2,1)}, u32[]{:S(2)}) copy-start(bf16[16,16,640]{2,1,0:T(8,128)(2,1)} %param.14) | copy-start | bytes 983044
  1.7 10.4 %copy-start.2 = (bf16[16,16,640]{2,1,0:T(8,128)(2,1)S(1)}, bf16[16,16,640]{2,1,0:T(8,128)(2,1)}, u32[]{:S(2)}) copy-start(bf16[16,16,640]{2,1,0:T(8,128)(2,1)} %param.15) | copy-start | bytes 983044
  1.7 10.4 %copy-start.4 = (bf16[32,640]{1,0:T(8,128)(2,1)S(1)}, bf16[32,640]{1,0:T(8,128)(2,1)}, u32[]{:S(2)}) copy-start(bf16[32,640]{1,0:T(8,128)(2,1)} %query.1) | copy-start | bytes 122884
  1.7 10.5 %copy-start.5 = (bf16[32,640]{1,0:T(8,128)(2,1)S(1)}, bf16[32,640]{1,0:T(8,128)(2,1)}, u32[]{:S(2)}) copy-start(bf16[32,640]{1,0:T(8,128)(2,1)} %new_key.1) | copy-start | bytes 122884
  1.7 10.5 %copy-start.6 = (bf16[32,640]{1,0:T(8,128)(2,1)S(1)}, bf16[32,640]{1,0:T(8,128)(2,1)}, u32[]{:S(2)}) copy-start(bf16[32,640]{1,0:T(8,128)(2,1)} %new_value.1) | copy-start | bytes 122884
  1.7 41.6 %all-to-all-start = ((bf16[4,80,640]{2,1,0:T(8,128)(2,1)}), bf16[4,80,640]{2,1,0:T(8,128)(2,1)S(1)}, u32[]{:S(2)}, u32[]{:S(2)}) async-start(bf16[4,80,640]{2,1,0:T(8,128)(2,1)} %broadcast_in_dim.2), calls=%async_computation | async-start | bytes 819200 | tf_op jit(solution)/shard_map/all_to_all | solution.py:185
  12.1 0.7 copy-start.7
  12.1 0.7 copy-start.8
  45.2 23.2 %all-to-all-start.1 = ((bf16[32,8,640]{2,1,0:T(8,128)(2,1)}), bf16[32,8,640]{2,1,0:T(8,128)(2,1)S(1)}, u32[]{:S(2)}, u32[]{:S(2)}) async-start(bf16[32,8,640]{2,1,0:T(8,128)(2,1)} %bitcast.4), calls=%async_computation.1 | async-start | bytes 655360 | tf_op jit(solution)/shard_map/all_to_all | solution.py:191
  59.2 0.7 copy-start.9
  59.9 8.6 %copy-start.3 = (bf16[4,64,80]{2,1,0:T(8,128)(2,1)S(1)}, bf16[4,64,80]{2,1,0:T(8,128)(2,1)}, u32[]{:S(2)}) copy-start(bf16[4,64,80]{2,1,0:T(8,128)(2,1)} %residual.1) | copy-start | bytes 122884
